TPU v7x, 128 devices: a whole 4x4x4 slice. The times are simulated.
128 devices in a mesh: role: 2 (over y_hi), dp: 4 (over y_lo, core), ctx: 16 (over x, z).
Axes of the slice: x: 4, y: 4 (y_hi: 2, y_lo: 2; y = y_hi * 2 + y_lo), z: 4, core: 2. Of those that a mesh axis runs over, the one named last changes fastest.
Arguments:
- teacher_states: bfloat16 [4, 2048, 5120], P('dp', 'ctx'), may hold values from -50 to 50
- student_states: bfloat16 [4, 2048, 3584], P('dp', 'ctx'), may hold values from -50 to 50
- teacher_gain: float32 [5120], replicated, may hold values from 0.25 to 1.75
- student_gain: float32 [3584], replicated, may hold values from 0.25 to 1.75
- mentor_output_weights: bfloat16 [4, 5120, 2048], P(None, None, 'ctx'), may hold values from -2 to 2
- student_heads: bfloat16 [4, 3584, 2048], P(None, None, 'ctx'), may hold values from -2 to 2
- segments: int32 [4, 2048], P('dp', 'ctx'), may hold values from 0 to 31, never falling along the last dimension, each value on 1 to 256 neighbouring positions
- targets: int32 [4, 2048, 4], P('dp', 'ctx'), may hold values from 0 to 2047
Outputs:
- grad_heads: float32 [4, 3584, 2048], P(None, ('role', 'dp'), 'ctx')
- frame_terms: float32 [2, 4, 2048, 4], P('role', 'dp', 'ctx')
All inputs are finite; a program needn't handle non-finite values.
Results may differ from a plain program's by a relative error of at most 0.0048.
Values may be sent and summed in bfloat16 or wider, within the bound.
No kernel may reach another device: no remote copies, remote signals or barrier semaphores. Data moves between devices by JAX's collectives and lax.ppermute only.
A program may use at most 192 MiB of HBM per device.

v0:
```python
import jax
import jax.numpy as jnp
from jax import lax
from jax.sharding import Mesh
from jax.sharding import PartitionSpec as P

QUANTIZER_TOTAL = 4
MBATCH = 4
CTX = ("ctx_0", "ctx_1")
epsilon = 1e-06
sharpness_divisor = 2.0
blend_ratio = 0.5


def sent_together(arrays, axis, dim, along):
    columns = [a.reshape(*a.shape[:along], -1) for a in arrays]
    both = jnp.concatenate(columns, axis=along)
    filled, at, done = (lax.all_gather(both, axis, axis=dim, tiled=True), 0, [])
    for a, column in zip(arrays, columns):
        share = filled[..., at : at + column.shape[along]]
        done.append(share.reshape(*share.shape[:along], *a.shape[along:]))
        at += column.shape[along]
    return tuple(done)


def copy_for_each(array, axis):
    copies = jnp.broadcast_to(array, (lax.axis_size(axis), *array.shape))
    return lax.all_to_all(copies, axis, split_axis=0, concat_axis=0, tiled=True)


def collected_together(array, axis):
    leaves = jax.tree.leaves(array)
    turns = sorted(range(len(leaves)), key=lambda k: -leaves[k].size)
    width = (1, *leaves[turns[0]].shape)[-1]
    lines = [
        jnp.pad(leaves[k].reshape(-1), (0, -leaves[k].size % width)).reshape(-1, width)
        for k in turns
    ]
    both, at, found = (copy_for_each(jnp.concatenate(lines), axis), 0, {})
    for k, line in zip(turns, lines):
        share = both[:, at : at + len(line)].reshape(len(both), -1)
        found[k] = share[:, : leaves[k].size].reshape(-1, *leaves[k].shape)
        at += len(line)
    numbers = iter(range(len(leaves)))
    return jax.tree.map(lambda _: found[next(numbers)], array)


def joined_by_halves(pieces, combine):
    while len(jax.tree.leaves(pieces)[0]) > 1:
        pieces = jax.vmap(combine)(
            *(jax.tree.map(lambda part: part[side::2], pieces) for side in (0, 1))
        )
    return jax.tree.map(lambda part: part[0], pieces)


def combined_all(array, axis, combine):
    pieces = collected_together(array, axis)
    return joined_by_halves(pieces, combine)


def cut_along(array, dim, length):
    lengths = array.shape
    pieces = array.reshape(*lengths[:dim], length, lengths[dim] // length, *lengths[dim + 1 :])
    return jnp.moveaxis(pieces, dim, 0)


def sum_at_owner(array, axis, dim):
    length = lax.axis_size(axis)
    pieces = lax.all_to_all(cut_along(array, dim, length), axis, 0, 0, tiled=True)
    return jnp.sum(pieces, axis=0)


def whole_of(array, axes, dim):
    filled = array
    for number in range(len(axes) - 1, -1, -1):
        filled = lax.all_gather(filled, axes[number], axis=dim, tiled=True)
    return filled


def shifted(value, axis, steps):
    count = lax.axis_size(axis)
    initial, last = (max(0, -steps), min(count, count - steps))
    return lax.ppermute(value, axis, [(source, source + steps) for source in range(initial, last)])


def normalize(states, gain):
    values = states.astype(jnp.float32)
    factor = lax.rsqrt(jnp.mean(values * values, axis=-1, keepdims=True) + epsilon)
    return (values * factor * gain).astype(jnp.bfloat16)


def merge_teacher(first, second):
    largest_activation = jnp.maximum(first[0], second[0])
    return (
        largest_activation,
        first[1] * jnp.exp(first[0] - largest_activation)
        + second[1] * jnp.exp(second[0] - largest_activation),
    )


def merge_student(first, second):
    largest_activation = jnp.maximum(first[0], second[0])
    return (
        largest_activation,
        first[1] * jnp.exp(first[0] - largest_activation)
        + second[1] * jnp.exp(second[0] - largest_activation),
        first[2] * jnp.exp((first[0] - largest_activation) / sharpness_divisor)
        + second[2] * jnp.exp((second[0] - largest_activation) / sharpness_divisor),
    )


def on_device(
    teacher_states,
    student_states,
    teacher_gain,
    student_gain,
    mentor_output_weights,
    student_heads,
    segments,
    targets,
):
    columns = mentor_output_weights.shape[2]
    ctx_count = lax.axis_size(CTX)
    ctx_rank = lax.axis_index(CTX)
    col_start = ctx_rank * columns
    rows_here = teacher_states.shape[1]
    batch_rows = rows_here // MBATCH
    group_rows = batch_rows * ctx_count
    all_segments, all_targets = sent_together((segments, targets), CTX, 1, 2)
    length = all_segments.shape[1]
    documents = 2 * ctx_count
    members = (all_segments[0][None, :] == jnp.arange(documents, dtype=jnp.int32)[:, None]).astype(
        jnp.float32
    )
    counts = jnp.sum(members, axis=1)
    row_sizes = jnp.dot(counts, members, precision=lax.Precision.HIGHEST)
    weights = length / (documents * row_sizes)
    own_targets = all_targets[0] - col_start
    is_teacher = lax.axis_index("role") == 0
    positions = jnp.arange(columns)

    def per_batch(values, batch_index):
        trailing = values.shape[1:]
        return values.reshape((ctx_count, MBATCH, batch_rows) + trailing)[:, batch_index].reshape(
            (group_rows,) + trailing
        )

    gradient = jnp.zeros((QUANTIZER_TOTAL, student_heads.shape[1], columns), jnp.float32)
    frame_parts = []
    blocks = []
    teacher_parts = []
    for batch_index in range(MBATCH):
        teacher_local_rows = normalize(
            teacher_states[0, batch_index * batch_rows : (batch_index + 1) * batch_rows],
            teacher_gain,
        )
        scaled = (
            lax.cond(
                is_teacher,
                lambda piece: jnp.einsum(
                    "rd,qdc->rqc", piece, mentor_output_weights, preferred_element_type=jnp.float32
                ),
                lambda piece: jnp.zeros((piece.shape[0], QUANTIZER_TOTAL, columns), jnp.float32),
                lax.all_gather(teacher_local_rows, CTX, axis=0, tiled=True),
            )
            / sharpness_divisor
        )
        teacher_local_peak = jnp.max(scaled, axis=2)
        teacher_largest_activation, totals = combined_all(
            (teacher_local_peak, jnp.sum(jnp.exp(scaled - teacher_local_peak[:, :, None]), axis=2)),
            CTX,
            merge_teacher,
        )
        log_probs = scaled - (teacher_largest_activation + jnp.log(totals))[:, :, None]
        teacher_hits = positions[None, None, :] == per_batch(own_targets, batch_index)[:, :, None]
        picked = -jnp.sum(jnp.where(teacher_hits, log_probs, 0.0), axis=2)
        teacher_terms = sum_at_owner(picked, CTX, 0)
        block = log_probs.astype(jnp.bfloat16)
        blocks.append(block)
        teacher_parts.append(teacher_terms)
    arrived = shifted(jnp.stack(blocks), "role", 1)
    for batch_index in range(MBATCH):
        received = arrived[batch_index]
        student_gradient = gradient
        local_rows = normalize(
            student_states[0, batch_index * batch_rows : (batch_index + 1) * batch_rows],
            student_gain,
        )
        gathered = whole_of(local_rows, CTX, 0)
        raw_activation_grid = lax.cond(
            is_teacher,
            lambda rows: jnp.zeros((rows.shape[0], QUANTIZER_TOTAL, columns), jnp.float32),
            lambda rows: jnp.einsum(
                "rd,qdc->rqc", rows, student_heads, preferred_element_type=jnp.float32
            ),
            gathered,
        )
        local_peak = jnp.max(raw_activation_grid, axis=2)
        centered_activations = raw_activation_grid - local_peak[:, :, None]
        largest_activation, plain, warmed_totals = combined_all(
            (
                local_peak,
                jnp.sum(jnp.exp(centered_activations), axis=2),
                jnp.sum(jnp.exp(centered_activations / sharpness_divisor), axis=2),
            ),
            CTX,
            merge_student,
        )
        untempered_logdensity = (
            raw_activation_grid - (largest_activation + jnp.log(plain))[:, :, None]
        )
        warmed_logdensity = (
            raw_activation_grid / sharpness_divisor
            - (largest_activation / sharpness_divisor + jnp.log(warmed_totals))[:, :, None]
        )
        teacher_logp = received.astype(jnp.float32)
        mentor_distribution = jnp.exp(teacher_logp)
        hits = (positions[None, None, :] == per_batch(own_targets, batch_index)[:, :, None]).astype(
            jnp.float32
        )
        kullback_gap = jnp.sum(mentor_distribution * (teacher_logp - warmed_logdensity), axis=2)
        mismatch_penalty = -jnp.sum(hits * untempered_logdensity, axis=2)
        loss_values = (
            blend_ratio * sharpness_divisor * sharpness_divisor * kullback_gap
            + (1.0 - blend_ratio) * mismatch_penalty
        )
        terms = sum_at_owner(loss_values, CTX, 0)
        gradient_scaling = per_batch(weights, batch_index)[:, None, None] * (
            blend_ratio * sharpness_divisor * (jnp.exp(warmed_logdensity) - mentor_distribution)
            + (1.0 - blend_ratio) * (jnp.exp(untempered_logdensity) - hits)
        )
        gradient_scaling = gradient_scaling.astype(jnp.bfloat16)
        student_gradient = lax.cond(
            is_teacher,
            lambda total: total,
            lambda total: total
            + jnp.einsum(
                "rd,rqc->qdc", gathered, gradient_scaling, preferred_element_type=jnp.float32
            ),
            student_gradient,
        )
        gradient = student_gradient
        frame_parts.append(jnp.where(is_teacher, teacher_parts[batch_index], terms))
    shares = lax.psum_scatter(gradient, ("role", "dp"), scatter_dimension=1, tiled=True)
    frame_terms = jnp.concatenate(frame_parts, axis=0).reshape(1, 1, rows_here, QUANTIZER_TOTAL)
    return (shares, frame_terms)


def solution(mesh):
    finer = Mesh(
        mesh.devices.reshape(mesh.shape["role"], mesh.shape["dp"], 4, 4),
        ("role", "dp", "ctx_0", "ctx_1"),
    )
    placed = (
        P("dp", CTX, None),
        P("dp", CTX, None),
        P(),
        P(),
        P(None, None, CTX),
        P(None, None, CTX),
        P("dp", CTX),
        P("dp", CTX, None),
    )
    return jax.shard_map(
        on_device,
        mesh=finer,
        in_specs=placed,
        out_specs=(P(None, ("role", "dp"), CTX), P("role", "dp", CTX, None)),
        check_vma=False,
    )
```

profile of v0, /device:TPU:24, one launch (start us, length us, event | category | flops | bytes accessed | tf_op | source)
XLA Modules:
  0.0 725.8 jit_solution(15006021371325651114)
XLA Ops:
  10.4 16.0 %all_gather.40 = bf16[128,3584]{1,0:T(8,128)(2,1)} all-gather(bf16[32,3584]{1,0:T(8,128)(2,1)S(1)} %get-tuple-element.260), channel_id=1, replica_groups=mesh['role'=2,'dp'=4,'ctx_0'=4,'ctx_1'=4] {'ctx_1'}, dimensions={0}, use_global_device_ids=true | all-gather | bytes 1146880 | tf_op jit(solution)/shard_map/all_gather | solution.py:76
  26.5 16.6 %all_gather.48 = bf16[128,3584]{1,0:T(8,128)(2,1)} all-gather(bf16[32,3584]{1,0:T(8,128)(2,1)S(1)} %get-tuple-element.259), channel_id=1, replica_groups=mesh['role'=2,'dp'=4,'ctx_0'=4,'ctx_1'=4] {'ctx_1'}, dimensions={0}, use_global_device_ids=true | all-gather | bytes 1146880 | tf_op jit(solution)/shard_map/all_gather | solution.py:76
  43.2 14.9 %all_gather.46 = bf16[128,3584]{1,0:T(8,128)(2,1)} all-gather(bf16[32,3584]{1,0:T(8,128)(2,1)S(1)} %get-tuple-element.258), channel_id=1, replica_groups=mesh['role'=2,'dp'=4,'ctx_0'=4,'ctx_1'=4] {'ctx_1'}, dimensions={0}, use_global_device_ids=true | all-gather | bytes 1146880 | tf_op jit(solution)/shard_map/all_gather | solution.py:76
  58.2 14.3 %all_gather.50 = bf16[128,3584]{1,0:T(8,128)(2,1)} all-gather(bf16[32,3584]{1,0:T(8,128)(2,1)S(1)} %get-tuple-element.257), channel_id=1, replica_groups=mesh['role'=2,'dp'=4,'ctx_0'=4,'ctx_1'=4] {'ctx_1'}, dimensions={0}, use_global_device_ids=true | all-gather | bytes 1146880 | tf_op jit(solution)/shard_map/all_gather | solution.py:76
  76.5 23.9 %all_gather.39 = s32[1,2048,5]{1,2,0:T(8,128)S(1)} all-gather(s32[1,128,5]{1,2,0:T(8,128)S(1)} %pad_add_fusion), channel_id=1, replica_groups=mesh['role'=2,'dp'=4,'ctx_0'=4,'ctx_1'=4] {'ctx_0','ctx_1'}, dimensions={1}, use_global_device_ids=true | all-gather | bytes 43520 | tf_op jit(solution)/shard_map/all_gather | solution.py:18
  106.8 11.3 %conditional.12 = (f32[512,4,128]{0,2,1:T(8,128)S(1)}, f32[512,4]{0,1:T(4,128)S(1)}) conditional(s32[]{:T(128)} %convert_element_type.149, (bf16[512,3584]{1,0:T(8,128)(2,1)}, bf16[4,3584,128]{2,1,0:T(8,128)(2,1)}) %tuple.96, () %tuple.97), branch_computations={%region_2.4_spmd, %region_4.0_spmd} | conditional | flops 1879308288 | bytes 16785424 | solution.py:190
  124.1 11.9 %conditional.18 = (f32[512,4,128]{0,2,1:T(8,128)S(1)}, f32[512,4]{0,1:T(4,128)S(1)}) conditional(s32[]{:T(128)} %convert_element_type.149, (bf16[512,3584]{1,0:T(8,128)(2,1)}, bf16[4,3584,128]{2,1,0:T(8,128)(2,1)}) %tuple.108, () %tuple.109), branch_computations={%region_34.36_spmd, %region_36.37_spmd} | conditional | flops 1879308288 | bytes 16785424 | solution.py:190
  136.0 30.0 %all-gather.19.cloned.1.call-done = bf16[512,3584]{1,0:T(8,128)(2,1)} async-done(((bf16[128,3584]{1,0:T(8,128)(2,1)}), bf16[512,3584]{1,0:T(8,128)(2,1)}) %all-gather.19.cloned.1.call-update) | async-done | bytes 3670032 | tf_op jit(solution)/shard_map/all_gather | solution.py:76
  166.0 13.5 %conditional.17 = (f32[512,4,128]{0,2,1:T(8,128)}, f32[512,4]{0,1:T(4,128)S(1)}) conditional(s32[]{:T(128)} %convert_element_type.149, (bf16[512,3584]{1,0:T(8,128)(2,1)}, bf16[4,3584,128]{2,1,0:T(8,128)(2,1)}) %tuple.106, () %tuple.107), branch_computations={%region_28.30_spmd, %region_30.31_spmd} | conditional | flops 1879308288 | bytes 16785424 | solution.py:190
  179.5 32.2 %all-gather.23.cloned.1.call-done = bf16[512,3584]{1,0:T(8,128)(2,1)} async-done(((bf16[128,3584]{1,0:T(8,128)(2,1)}), bf16[512,3584]{1,0:T(8,128)(2,1)}) %all-gather.23.cloned.1.call-update) | async-done | bytes 3670032 | tf_op jit(solution)/shard_map/all_gather | solution.py:76
  211.7 11.7 %conditional.19 = (f32[512,4,128]{0,2,1:T(8,128)S(1)}, f32[512,4]{0,1:T(4,128)S(1)}) conditional(s32[]{:T(128)} %convert_element_type.149, (bf16[512,3584]{1,0:T(8,128)(2,1)}, bf16[4,3584,128]{2,1,0:T(8,128)(2,1)}) %tuple.110, () %tuple.111), branch_computations={%region_40.42_spmd, %region_42.43_spmd} | conditional | flops 1879308288 | bytes 16785424 | solution.py:190
  264.9 11.1 %all-gather.13.cloned.1.call-done = bf16[512,5120]{1,0:T(8,128)(2,1)} async-done(((bf16[32,5120]{1,0:T(8,128)(2,1)}), bf16[512,5120]{1,0:T(8,128)(2,1)}) %all-gather.13.cloned.1.call-update) | async-done | bytes 5242896 | tf_op jit(solution)/shard_map/all_gather | solution.py:164
  277.1 57.0 %all-gather.15.cloned.1.call-done = bf16[512,5120]{1,0:T(8,128)(2,1)} async-done(((bf16[32,5120]{1,0:T(8,128)(2,1)}), bf16[512,5120]{1,0:T(8,128)(2,1)}) %all-gather.15.cloned.1.call-update) | async-done | bytes 5242896 | tf_op jit(solution)/shard_map/all_gather | solution.py:164
  335.3 57.1 %all-gather.17.cloned.1.call-done = bf16[512,5120]{1,0:T(8,128)(2,1)} async-done(((bf16[32,5120]{1,0:T(8,128)(2,1)}), bf16[512,5120]{1,0:T(8,128)(2,1)}) %all-gather.17.cloned.1.call-update) | async-done | bytes 5242896 | tf_op jit(solution)/shard_map/all_gather | solution.py:164
  396.3 54.3 %all-gather.11.cloned.1.call-done = bf16[512,5120]{1,0:T(8,128)(2,1)} async-done(((bf16[32,5120]{1,0:T(8,128)(2,1)}), bf16[512,5120]{1,0:T(8,128)(2,1)}) %all-gather.11.cloned.1.call-update) | async-done | bytes 5242896 | tf_op jit(solution)/shard_map/all_gather | solution.py:164
  460.8 8.5 %all-to-all-done.4 = f32[16,1024,4]{1,2,0:T(4,128)S(1)} async-done(((f32[16,1024,4]{1,2,0:T(4,128)}), f32[16,1024,4]{1,2,0:T(4,128)S(1)}, u32[]{:S(2)}, u32[]{:S(2)}) %all-to-all-start.4) | async-done | bytes 262176 | tf_op jit(solution)/shard_map/all_to_all | solution.py:28
  524.1 46.9 %collective-permute-done = bf16[4,512,4,128]{1,3,2,0:T(8,128)(2,1)} collective-permute-done((bf16[4,512,4,128]{1,3,2,0:T(8,128)(2,1)}, bf16[4,512,4,128]{1,3,2,0:T(8,128)(2,1)}, u32[]{:S(2)}, u32[]{:S(2)}) %collective-permute-start) | collective-permute-done | bytes 2097184 | tf_op jit(solution)/shard_map/ppermute | solution.py:83
  580.8 9.7 %conditional.21 = (f32[4,3584,128]{1,2,0:T(8,128)}) conditional(s32[]{:T(128)} %convert_element_type.149, (bf16[512,4,128]{0,2,1:T(8,128)(2,1)}, bf16[512,3584]{1,0:T(8,128)(2,1)}, f32[4,3584,128]{1,2,0:T(8,128)}) %tuple.114, f32[4,3584,128]{1,2,0:T(8,128)} %get-tuple-element.317), branch_computations={%region_47.48_spmd, %region_48.49_spmd} | conditional | flops 1880883200 | bytes 18874376 | solution.py:233
  581.0 9.5 %bitcast_add_fusion = f32[4,3584,128]{1,2,0:T(8,128)} fusion(f32[4,3584,128]{1,2,0:T(8,128)} %get-tuple-element.107, bf16[512,4,128]{0,2,1:T(8,128)(2,1)} %get-tuple-element.108, bf16[512,3584]{1,0:T(8,128)(2,1)} %get-tuple-element.109), kind=kOutput, calls=%fused_computation.10 | convolution fusion | flops 1880883200 | bytes 18874368 | tf_op jit(solution)/shard_map/cond/branch_0_fun/rd,rqc->qdc/dot_general | solution.py:237
  590.5 9.5 %conditional.22 = (f32[4,3584,128]{1,2,0:T(8,128)}) conditional(s32[]{:T(128)} %convert_element_type.149, (bf16[512,4,128]{0,2,1:T(8,128)(2,1)}, bf16[512,3584]{1,0:T(8,128)(2,1)}, f32[4,3584,128]{1,2,0:T(8,128)}) %tuple.115, f32[4,3584,128]{1,2,0:T(8,128)} %get-tuple-element.318), branch_computations={%region_49.50_spmd, %region_50.51_spmd} | conditional | flops 1880883200 | bytes 18874376 | solution.py:233
  590.5 9.5 %bitcast_add_fusion.1 = f32[4,3584,128]{1,2,0:T(8,128)} fusion(f32[4,3584,128]{1,2,0:T(8,128)} %get-tuple-element.110, bf16[512,4,128]{0,2,1:T(8,128)(2,1)} %get-tuple-element.111, bf16[512,3584]{1,0:T(8,128)(2,1)} %get-tuple-element.112), kind=kOutput, calls=%fused_computation.12 | convolution fusion | flops 1880883200 | bytes 18874368 | tf_op jit(solution)/shard_map/cond/branch_0_fun/rd,rqc->qdc/dot_general | solution.py:237
  601.7 9.4 %conditional.23 = (f32[4,3584,128]{1,2,0:T(8,128)}) conditional(s32[]{:T(128)} %convert_element_type.149, (bf16[512,4,128]{0,2,1:T(8,128)(2,1)S(1)}, bf16[512,3584]{1,0:T(8,128)(2,1)}, f32[4,3584,128]{1,2,0:T(8,128)}) %tuple.116, f32[4,3584,128]{1,2,0:T(8,128)} %get-tuple-element.319), branch_computations={%region_51.52_spmd, %region_52.53_spmd} | conditional | flops 1880883200 | bytes 18874376 | solution.py:233
  601.7 9.4 %bitcast_add_fusion.2 = f32[4,3584,128]{1,2,0:T(8,128)} fusion(f32[4,3584,128]{1,2,0:T(8,128)} %get-tuple-element.113, bf16[512,4,128]{0,2,1:T(8,128)(2,1)S(1)} %get-tuple-element.114, bf16[512,3584]{1,0:T(8,128)(2,1)} %get-tuple-element.115), kind=kOutput, calls=%fused_computation.14 | convolution fusion | flops 1880883200 | bytes 18874368 | tf_op jit(solution)/shard_map/cond/branch_0_fun/rd,rqc->qdc/dot_general | solution.py:237
  611.1 8.4 %copy.52 = f32[4,3584,128]{2,1,0:T(8,128)} copy(f32[4,3584,128]{1,2,0:T(8,128)} %get-tuple-element.320) | data formatting | bytes 14680064 | tf_op jit(solution)/shard_map/cond | solution.py:233
  (333 shorter events, 297.9 us)
Async XLA Ops:
  7.2 99.6 %all-gather.9.cloned.1.call-start = ((), (), s32[]{:S(2)}) async-start(), calls=%async_computation.17 | async-start | bytes 4587520 | tf_op jit(solution)/shard_map/all_gather | solution.py:76
  26.4 97.7 %all-gather.21.cloned.1.call-start = ((), (), s32[]{:S(2)}) async-start(), calls=%async_computation.23 | async-start | bytes 4587520 | tf_op jit(solution)/shard_map/all_gather | solution.py:76
  43.1 122.9 %all-gather.19.cloned.1.call-start = ((), (), s32[]{:S(2)}) async-start(), calls=%async_computation.22 | async-start | bytes 4587520 | tf_op jit(solution)/shard_map/all_gather | solution.py:76
  58.1 153.6 %all-gather.23.cloned.1.call-start = ((), (), s32[]{:S(2)}) async-start(), calls=%async_computation.24 | async-start | bytes 4587520 | tf_op jit(solution)/shard_map/all_gather | solution.py:76
  72.5 203.5 %all-gather.13.cloned.1.call-start = ((), (), s32[]{:S(2)}) async-start(), calls=%async_computation.19 | async-start | bytes 5570560 | tf_op jit(solution)/shard_map/all_gather | solution.py:164
  74.4 259.7 %all-gather.15.cloned.1.call-start = ((), (), s32[]{:S(2)}) async-start(), calls=%async_computation.20 | async-start | bytes 5570560 | tf_op jit(solution)/shard_map/all_gather | solution.py:164
  75.0 317.4 %all-gather.17.cloned.1.call-start = ((), (), s32[]{:S(2)}) async-start(), calls=%async_computation.21 | async-start | bytes 5570560 | tf_op jit(solution)/shard_map/all_gather | solution.py:164
  75.7 374.9 %all-gather.11.cloned.1.call-start = ((), (), s32[]{:S(2)}) async-start(), calls=%async_computation.18 | async-start | bytes 5570560 | tf_op jit(solution)/shard_map/all_gather | solution.py:164
  119.2 108.2 %all-to-all-start = ((f32[16,1536,4]{1,2,0:T(4,128)}), f32[16,1536,4]{1,2,0:T(4,128)S(1)}, u32[]{:S(2)}, u32[]{:S(2)}) async-start(f32[16,1536,4]{1,2,0:T(4,128)} %broadcast_in_dim.25), calls=%async_computation | async-start | bytes 786432 | tf_op jit(solution)/shard_map/all_to_all | solution.py:28
  229.0 15.9 %all-to-all-start.7 = ((f32[16,1536,4]{1,2,0:T(4,128)}), f32[16,1536,4]{1,2,0:T(4,128)}, u32[]{:S(2)}, u32[]{:S(2)}) async-start(f32[16,1536,4]{1,2,0:T(4,128)} %broadcast_in_dim.32), calls=%async_computation.7 | async-start | bytes 786432 | tf_op jit(solution)/shard_map/all_to_all | solution.py:28
  246.4 17.0 %all-to-all-start.6 = ((f32[16,1536,4]{1,2,0:T(4,128)}), f32[16,1536,4]{1,2,0:T(4,128)S(1)}, u32[]{:S(2)}, u32[]{:S(2)}) async-start(f32[16,1536,4]{1,2,0:T(4,128)} %broadcast_in_dim.31), calls=%async_computation.6 | async-start | bytes 786432 | tf_op jit(solution)/shard_map/all_to_all | solution.py:28
  455.5 13.8 %all-to-all-start.4 = ((f32[16,1024,4]{1,2,0:T(4,128)}), f32[16,1024,4]{1,2,0:T(4,128)S(1)}, u32[]{:S(2)}, u32[]{:S(2)}) async-start(f32[16,1024,4]{1,2,0:T(4,128)} %broadcast_in_dim.29), calls=%async_computation.4 | async-start | bytes 524288 | tf_op jit(solution)/shard_map/all_to_all | solution.py:28
  470.1 12.2 %all-to-all-start.3 = ((f32[16,1024,4]{1,2,0:T(4,128)}), f32[16,1024,4]{1,2,0:T(4,128)S(1)}, u32[]{:S(2)}, u32[]{:S(2)}) async-start(f32[16,1024,4]{1,2,0:T(4,128)} %broadcast_in_dim.28), calls=%async_computation.3 | async-start | bytes 524288 | tf_op jit(solution)/shard_map/all_to_all | solution.py:28
  483.1 12.1 %all-to-all-start.2 = ((f32[16,1024,4]{1,2,0:T(4,128)}), f32[16,1024,4]{1,2,0:T(4,128)S(1)}, u32[]{:S(2)}, u32[]{:S(2)}) async-start(f32[16,1024,4]{1,2,0:T(4,128)} %broadcast_in_dim.27), calls=%async_computation.2 | async-start | bytes 524288 | tf_op jit(solution)/shard_map/all_to_all | solution.py:28
  496.1 12.1 %all-to-all-start.1 = ((f32[16,1024,4]{1,2,0:T(4,128)}), f32[16,1024,4]{1,2,0:T(4,128)S(1)}, u32[]{:S(2)}, u32[]{:S(2)}) async-start(f32[16,1024,4]{1,2,0:T(4,128)} %broadcast_in_dim.26), calls=%async_computation.1 | async-start | bytes 524288 | tf_op jit(solution)/shard_map/all_to_all | solution.py:28
  509.1 14.7 %all-to-all-start.5 = ((f32[16,1536,4]{1,2,0:T(4,128)}), f32[16,1536,4]{1,2,0:T(4,128)S(1)}, u32[]{:S(2)}, u32[]{:S(2)}) async-start(f32[16,1536,4]{1,2,0:T(4,128)} %broadcast_in_dim.30), calls=%async_computation.5 | async-start | bytes 786432 | tf_op jit(solution)/shard_map/all_to_all | solution.py:28
  514.6 204.4 %reduce-scatter.2.cloned.1.call-start = ((), (), s32[]{:S(2)}) async-start(), calls=%async_computation.25 | async-start | bytes 8257536 | tf_op jit(solution)/shard_map/reduce_scatter | solution.py:244
  519.9 51.2 %collective-permute-start = (bf16[4,512,4,128]{1,3,2,0:T(8,128)(2,1)}, bf16[4,512,4,128]{1,3,2,0:T(8,128)(2,1)}, u32[]{:S(2)}, u32[]{:S(2)}) collective-permute-start(bf16[4,512,4,128]{1,3,2,0:T(8,128)(2,1)} %pad_maximum_fusion), channel_id=1, source_target_pairs={{0,64},{1,65},{2,66},{3,67},{4,68},{5,69},{6,70},{7,71},{8,72},{9,... | collective-permute-start | bytes 6291464 | tf_op jit(solution)/shard_map/ppermute | solution.py:83
  621.0 14.5 %all-to-all-start.14 = ((f32[16,1,128]{2,1,0:T(1,128)}), f32[16,1,128]{2,1,0:T(1,128)S(1)}, u32[]{:S(2)}, u32[]{:S(2)}) async-start(f32[16,1,128]{2,1,0:T(1,128)} %reshape.455), calls=%async_computation.15 | async-start | bytes 16384 | tf_op jit(solution)/shard_map/all_to_all | solution.py:69
  635.5 10.9 %all-to-all-start.12 = ((f32[16,1,128]{2,1,0:T(1,128)}), f32[16,1,128]{2,1,0:T(1,128)S(1)}, u32[]{:S(2)}, u32[]{:S(2)}) async-start(f32[16,1,128]{2,1,0:T(1,128)} %reshape.459), calls=%async_computation.13 | async-start | bytes 16384 | tf_op jit(solution)/shard_map/all_to_all | solution.py:69
  657.3 10.9 %all-to-all-start.8 = ((f32[16,1,128]{2,1,0:T(1,128)}), f32[16,1,128]{2,1,0:T(1,128)S(1)}, u32[]{:S(2)}, u32[]{:S(2)}) async-start(f32[16,1,128]{2,1,0:T(1,128)} %reshape.467), calls=%async_computation.9 | async-start | bytes 16384 | tf_op jit(solution)/shard_map/all_to_all | solution.py:69
  673.7 11.0 %all-to-all-start.15 = ((f32[16,1,128]{2,1,0:T(1,128)}), f32[16,1,128]{2,1,0:T(1,128)S(1)}, u32[]{:S(2)}, u32[]{:S(2)}) async-start(f32[16,1,128]{2,1,0:T(1,128)} %reshape.457), calls=%async_computation.16 | async-start | bytes 16384 | tf_op jit(solution)/shard_map/all_to_all | solution.py:69
  684.7 10.9 %all-to-all-start.13 = ((f32[16,1,128]{2,1,0:T(1,128)}), f32[16,1,128]{2,1,0:T(1,128)S(1)}, u32[]{:S(2)}, u32[]{:S(2)}) async-start(f32[16,1,128]{2,1,0:T(1,128)} %reshape.461), calls=%async_computation.14 | async-start | bytes 16384 | tf_op jit(solution)/shard_map/all_to_all | solution.py:69
  695.6 11.0 %all-to-all-start.11 = ((f32[16,1,128]{2,1,0:T(1,128)}), f32[16,1,128]{2,1,0:T(1,128)S(1)}, u32[]{:S(2)}, u32[]{:S(2)}) async-start(f32[16,1,128]{2,1,0:T(1,128)} %reshape.465), calls=%async_computation.12 | async-start | bytes 16384 | tf_op jit(solution)/shard_map/all_to_all | solution.py:69
  (42 other events, 664.2 us)
Sparse Core Ops, SparseCore 0:
  26.5 45.5 all-gather.8
  73.8 46.2 all-gather.20
  121.8 44.1 all-gather.18
  167.5 44.1 all-gather.22
  213.7 62.2 all-gather.12
  278.0 56.0 all-gather.14
  336.3 56.0 all-gather.16
  394.6 56.0 all-gather.10
  619.7 46.5 reduce-scatter.1
where the time goes:
time: 736 us; the launch traced here: 726 us
  waiting for transfers between devices  378 us (51%)
  blocking collectives  85.7 us (12%)
  starting transfers between devices  69.3 us (9%)
  local copies, waits for them, and re-layouts  65.5 us (9%)
  matrix products  56.1 us (8%)
  other arithmetic  54.6 us (7%)
  between operations  15.2 us (2%)
    all_gather x4, waiting for transfers between devices, on_device(): lax.all_gather(teacher_local_rows, CTX, axis=0, tiled=True)  180 us
    all_gather x4, waiting for transfers between devices, whole_of(): filled = lax.all_gather(filled, axes[number], axis=dim, tiled=True)  62.2 us
    all_gather x4, blocking collectives, whole_of(): filled = lax.all_gather(filled, axes[number], axis=dim, tiled=True)  61.8 us
    all_to_all x8, waiting for transfers between devices, sum_at_owner(): lax.all_to_all(cut_along(array, dim, length), axis, 0, 0, tiled=True)  49.9 us
    ppermute x1, waiting for transfers between devices, shifted(): lax.ppermute(value, axis, [(source, source + steps) for source in range(i...  46.9 us
    all_to_all x8, waiting for transfers between devices, copy_for_each(): return lax.all_to_all(copies, axis, split_axis=0, concat_axis=0, tiled=True)  37.9 us
    all_to_all x8, starting transfers between devices, copy_for_each(): return lax.all_to_all(copies, axis, split_axis=0, concat_axis=0, tiled=True)  36.6 us
    dot_general x4, matrix products, on_device(): jnp.einsum('rd,rqc->qdc', gathered, gradient_scaling, preferred_element_t...  33.5 us
  transfers between devices with their start and end apart: 26, of which 22 were waited for; matrix products, arithmetic and copies ran while one was open for 16% of the time, Pallas kernels for 0%

commit v1 on v0

--- a/solution.py
+++ b/solution.py
@@ -161,7 +161,10 @@
                     "rd,qdc->rqc", piece, mentor_output_weights, preferred_element_type=jnp.float32
                 ),
                 lambda piece: jnp.zeros((piece.shape[0], QUANTIZER_TOTAL, columns), jnp.float32),
-                lax.all_gather(teacher_local_rows, CTX, axis=0, tiled=True),
+                jnp.concatenate(
+                    lax.all_to_all(jnp.stack([teacher_local_rows] * lax.axis_size(CTX)), CTX, 0, 0),
+                    axis=0,
+                ),
             )
             / sharpness_divisor
         )

time: 736 us -> 817 us (1.11)
  blocking collectives: 85.7 us -> 273 us
  waiting for transfers between devices: 378 us -> 250 us
  starting transfers between devices: 69.3 us -> 104 us
  other arithmetic: 54.6 us -> 39.7 us
    all_gather x4 -> x0, waiting for transfers between devices: 180 us -> none  [on_device(): lax.all_gather(teacher_local_rows, CTX, axis=0, tiled=True)]
    all_gather x4, blocking collectives: 61.8 us -> 193 us  [whole_of(): filled = lax.all_gather(filled, axes[number], axis=dim, tiled=True)]
    all_to_all x0 -> x4, waiting for transfers between devices: none -> 120 us  [on_device(): lax.all_to_all(jnp.stack([teacher_local_rows] * lax.axis_size(CTX)), CTX,...]
    all_gather x4, waiting for transfers between devices: 62.2 us -> 0.04 us  [whole_of(): filled = lax.all_gather(filled, axes[number], axis=dim, tiled=True)]
    all_gather x1, blocking collectives: 23.9 us -> 79.5 us  [sent_together(): filled, at, done = (lax.all_gather(both, axis, axis=dim, tiled=True), 0, [])]
    all_to_all x0 -> x4, starting transfers between devices: none -> 38.1 us  [on_device(): lax.all_to_all(jnp.stack([teacher_local_rows] * lax.axis_size(CTX)), CTX,...]
    ppermute x1, waiting for transfers between devices: 46.9 us -> 32.9 us  [shifted(): lax.ppermute(value, axis, [(source, source + steps) for source in range(i...]
    another operation x8 -> x12, local copies, waits for them, and re-layouts: 26.3 us -> 36.2 us
  transfers between devices with their start and end apart: 26 -> 26, of which waited for: 22 -> 19; matrix products, arithmetic and copies ran while one was open for 16% -> 13% of each run, Pallas kernels for 0% -> 0%
where the time goes in v1:
time: 817 us; the launch traced here: 807 us
  blocking collectives  273 us (33%)
  waiting for transfers between devices  250 us (31%)
  starting transfers between devices  104 us (13%)
  local copies, waits for them, and re-layouts  69.4 us (8%)
  matrix products  54.6 us (7%)
  other arithmetic  39.7 us (5%)
  between operations  15.3 us (2%)
    all_gather x4, blocking collectives, whole_of(): filled = lax.all_gather(filled, axes[number], axis=dim, tiled=True)  193 us
    all_to_all x4, waiting for transfers between devices, on_device(): lax.all_to_all(jnp.stack([teacher_local_rows] * lax.axis_size(CTX)), CTX,...  120 us
    all_gather x1, blocking collectives, sent_together(): filled, at, done = (lax.all_gather(both, axis, axis=dim, tiled=True), 0, [])  79.5 us
    all_to_all x8, waiting for transfers between devices, sum_at_owner(): lax.all_to_all(cut_along(array, dim, length), axis, 0, 0, tiled=True)  51.6 us
    all_to_all x8, waiting for transfers between devices, copy_for_each(): return lax.all_to_all(copies, axis, split_axis=0, concat_axis=0, tiled=True)  45.4 us
    all_to_all x4, starting transfers between devices, on_device(): lax.all_to_all(jnp.stack([teacher_local_rows] * lax.axis_size(CTX)), CTX,...  38.1 us
    dot_general x4, matrix products, on_device(): jnp.einsum('rd,rqc->qdc', gathered, gradient_scaling, preferred_element_t...  33.5 us
    all_to_all x8, starting transfers between devices, copy_for_each(): return lax.all_to_all(copies, axis, split_axis=0, concat_axis=0, tiled=True)  33.3 us
  transfers between devices with their start and end apart: 26, of which 19 were waited for; matrix products, arithmetic and copies ran while one was open for 13% of the time, Pallas kernels for 0%

profile of v1, /device:TPU:24, one launch (start us, length us, event | category | flops | bytes accessed | tf_op | source)
XLA Modules:
  0.0 806.8 jit_solution(10987410289568129229)
XLA Ops:
  22.3 67.1 %all_gather.28 = bf16[128,3584]{1,0:T(8,128)(2,1)} all-gather(bf16[32,3584]{1,0:T(8,128)(2,1)S(1)} %get-tuple-element.264), channel_id=1, replica_groups=mesh['role'=2,'dp'=4,'ctx_0'=4,'ctx_1'=4] {'ctx_1'}, dimensions={0}, use_global_device_ids=true | all-gather | bytes 1146880 | tf_op jit(solution)/shard_map/all_gather | solution.py:76
  89.4 11.2 %all-to-all-done.1 = bf16[16,32,5120]{2,1,0:T(8,128)(2,1)} async-done(((bf16[16,32,5120]{2,1,0:T(8,128)(2,1)}), bf16[16,32,5120]{2,1,0:T(8,128)(2,1)}, u32[]{:S(2)}, u32[]{:S(2)}) %all-to-all-start.1) | async-done | bytes 5242912 | tf_op jit(solution)/shard_map/all_to_all | solution.py:165
  103.6 12.3 %all-to-all-start.3 = ((bf16[16,32,5120]{2,1,0:T(8,128)(2,1)}), bf16[16,32,5120]{2,1,0:T(8,128)(2,1)}, u32[]{:S(2)}, u32[]{:S(2)}) async-start(bf16[16,32,5120]{2,1,0:T(8,128)(2,1)} %stack.30), calls=%async_computation.3 | async-start | bytes 10485760 | tf_op jit(solution)/shard_map/all_to_all | solution.py:165
  116.0 42.6 %all_gather.32 = bf16[128,3584]{1,0:T(8,128)(2,1)} all-gather(bf16[32,3584]{1,0:T(8,128)(2,1)S(1)} %get-tuple-element.263), channel_id=1, replica_groups=mesh['role'=2,'dp'=4,'ctx_0'=4,'ctx_1'=4] {'ctx_1'}, dimensions={0}, use_global_device_ids=true | all-gather | bytes 1146880 | tf_op jit(solution)/shard_map/all_gather | solution.py:76
  158.6 48.9 %all-to-all-done.3 = bf16[16,32,5120]{2,1,0:T(8,128)(2,1)} async-done(((bf16[16,32,5120]{2,1,0:T(8,128)(2,1)}), bf16[16,32,5120]{2,1,0:T(8,128)(2,1)}, u32[]{:S(2)}, u32[]{:S(2)}) %all-to-all-start.3) | async-done | bytes 5242912 | tf_op jit(solution)/shard_map/all_to_all | solution.py:165
  210.4 10.0 %all-to-all-start.5 = ((bf16[16,32,5120]{2,1,0:T(8,128)(2,1)}), bf16[16,32,5120]{2,1,0:T(8,128)(2,1)}, u32[]{:S(2)}, u32[]{:S(2)}) async-start(bf16[16,32,5120]{2,1,0:T(8,128)(2,1)} %stack.33), calls=%async_computation.5 | async-start | bytes 10485760 | tf_op jit(solution)/shard_map/all_to_all | solution.py:165
  220.5 41.6 %all_gather.30 = bf16[128,3584]{1,0:T(8,128)(2,1)} all-gather(bf16[32,3584]{1,0:T(8,128)(2,1)S(1)} %get-tuple-element.262), channel_id=1, replica_groups=mesh['role'=2,'dp'=4,'ctx_0'=4,'ctx_1'=4] {'ctx_1'}, dimensions={0}, use_global_device_ids=true | all-gather | bytes 1146880 | tf_op jit(solution)/shard_map/all_gather | solution.py:76
  262.2 59.9 %all-to-all-done.5 = bf16[16,32,5120]{2,1,0:T(8,128)(2,1)} async-done(((bf16[16,32,5120]{2,1,0:T(8,128)(2,1)}), bf16[16,32,5120]{2,1,0:T(8,128)(2,1)}, u32[]{:S(2)}, u32[]{:S(2)}) %all-to-all-start.5) | async-done | bytes 5242912 | tf_op jit(solution)/shard_map/all_to_all | solution.py:165
  332.7 42.2 %all_gather.34 = bf16[128,3584]{1,0:T(8,128)(2,1)} all-gather(bf16[32,3584]{1,0:T(8,128)(2,1)S(1)} %get-tuple-element.261), channel_id=1, replica_groups=mesh['role'=2,'dp'=4,'ctx_0'=4,'ctx_1'=4] {'ctx_1'}, dimensions={0}, use_global_device_ids=true | all-gather | bytes 1146880 | tf_op jit(solution)/shard_map/all_gather | solution.py:76
  374.9 79.5 %all_gather.27 = s32[1,2048,5]{1,2,0:T(8,128)S(1)} all-gather(s32[1,128,5]{1,2,0:T(8,128)S(1)} %pad_add_fusion), channel_id=1, replica_groups=mesh['role'=2,'dp'=4,'ctx_0'=4,'ctx_1'=4] {'ctx_0','ctx_1'}, dimensions={1}, use_global_device_ids=true | all-gather | bytes 43520 | tf_op jit(solution)/shard_map/all_gather | solution.py:18
  479.0 8.4 %all-to-all-done.6 = f32[16,1024,4]{1,2,0:T(4,128)} async-done(((f32[16,1024,4]{1,2,0:T(4,128)}), f32[16,1024,4]{1,2,0:T(4,128)}, u32[]{:S(2)}, u32[]{:S(2)}) %all-to-all-start.6) | async-done | bytes 262176 | tf_op jit(solution)/shard_map/all_to_all | solution.py:28
  514.0 11.3 %conditional.12 = (f32[512,4,128]{0,2,1:T(8,128)S(1)}, f32[512,4]{0,1:T(4,128)S(1)}) conditional(s32[]{:T(128)} %convert_element_type.149, (bf16[512,3584]{1,0:T(8,128)(2,1)}, bf16[4,3584,128]{2,1,0:T(8,128)(2,1)}) %tuple.96, () %tuple.97), branch_computations={%region_2.4_spmd, %region_4.0_spmd} | conditional | flops 1879308288 | bytes 16785424 | solution.py:193
  530.1 11.3 %conditional.18 = (f32[512,4,128]{0,2,1:T(8,128)S(1)}, f32[512,4]{0,1:T(4,128)S(1)}) conditional(s32[]{:T(128)} %convert_element_type.149, (bf16[512,3584]{1,0:T(8,128)(2,1)}, bf16[4,3584,128]{2,1,0:T(8,128)(2,1)}) %tuple.108, () %tuple.109), branch_computations={%region_34.36_spmd, %region_36.37_spmd} | conditional | flops 1879308288 | bytes 16785424 | solution.py:193
  541.5 11.5 %conditional.17 = (f32[512,4,128]{0,2,1:T(8,128)S(1)}, f32[512,4]{0,1:T(4,128)S(1)}) conditional(s32[]{:T(128)} %convert_element_type.149, (bf16[512,3584]{1,0:T(8,128)(2,1)}, bf16[4,3584,128]{2,1,0:T(8,128)(2,1)}) %tuple.106, () %tuple.107), branch_computations={%region_28.30_spmd, %region_30.31_spmd} | conditional | flops 1879308288 | bytes 16785424 | solution.py:193
  554.9 11.3 %conditional.19 = (f32[512,4,128]{0,2,1:T(8,128)S(1)}, f32[512,4]{0,1:T(4,128)S(1)}) conditional(s32[]{:T(128)} %convert_element_type.149, (bf16[512,3584]{1,0:T(8,128)(2,1)}, bf16[4,3584,128]{2,1,0:T(8,128)(2,1)}) %tuple.110, () %tuple.111), branch_computations={%region_40.42_spmd, %region_42.43_spmd} | conditional | flops 1879308288 | bytes 16785424 | solution.py:193
  577.4 10.0 %all-to-all-done.10 = f32[16,1536,4]{1,2,0:T(4,128)} async-done(((f32[16,1536,4]{1,2,0:T(4,128)}), f32[16,1536,4]{1,2,0:T(4,128)}, u32[]{:S(2)}, u32[]{:S(2)}) %all-to-all-start.10) | async-done | bytes 393248 | tf_op jit(solution)/shard_map/all_to_all | solution.py:28
  617.6 32.9 %collective-permute-done = bf16[4,512,4,128]{1,3,2,0:T(8,128)(2,1)} collective-permute-done((bf16[4,512,4,128]{1,3,2,0:T(8,128)(2,1)}, bf16[4,512,4,128]{1,3,2,0:T(8,128)(2,1)}, u32[]{:S(2)}, u32[]{:S(2)}) %collective-permute-start) | collective-permute-done | bytes 2097184 | tf_op jit(solution)/shard_map/ppermute | solution.py:83
  660.2 9.7 %conditional.21 = (f32[4,3584,128]{1,2,0:T(8,128)}) conditional(s32[]{:T(128)} %convert_element_type.149, (bf16[512,4,128]{0,2,1:T(8,128)(2,1)}, bf16[512,3584]{1,0:T(8,128)(2,1)}, f32[4,3584,128]{1,2,0:T(8,128)}) %tuple.114, f32[4,3584,128]{1,2,0:T(8,128)} %get-tuple-element.321), branch_computations={%region_47.48_spmd, %region_48.49_spmd} | conditional | flops 1880883200 | bytes 18874376 | solution.py:236
  660.4 9.5 %bitcast_add_fusion = f32[4,3584,128]{1,2,0:T(8,128)} fusion(f32[4,3584,128]{1,2,0:T(8,128)} %get-tuple-element.111, bf16[512,4,128]{0,2,1:T(8,128)(2,1)} %get-tuple-element.112, bf16[512,3584]{1,0:T(8,128)(2,1)} %get-tuple-element.113), kind=kOutput, calls=%fused_computation.2 | convolution fusion | flops 1880883200 | bytes 18874368 | tf_op jit(solution)/shard_map/cond/branch_0_fun/rd,rqc->qdc/dot_general | solution.py:240
  669.9 9.5 %conditional.22 = (f32[4,3584,128]{1,2,0:T(8,128)}) conditional(s32[]{:T(128)} %convert_element_type.149, (bf16[512,4,128]{0,2,1:T(8,128)(2,1)}, bf16[512,3584]{1,0:T(8,128)(2,1)}, f32[4,3584,128]{1,2,0:T(8,128)}) %tuple.115, f32[4,3584,128]{1,2,0:T(8,128)} %get-tuple-element.322), branch_computations={%region_49.50_spmd, %region_50.51_spmd} | conditional | flops 1880883200 | bytes 18874376 | solution.py:236
  669.9 9.5 %bitcast_add_fusion.1 = f32[4,3584,128]{1,2,0:T(8,128)} fusion(f32[4,3584,128]{1,2,0:T(8,128)} %get-tuple-element.114, bf16[512,4,128]{0,2,1:T(8,128)(2,1)} %get-tuple-element.115, bf16[512,3584]{1,0:T(8,128)(2,1)} %get-tuple-element.116), kind=kOutput, calls=%fused_computation.4 | convolution fusion | flops 1880883200 | bytes 18874368 | tf_op jit(solution)/shard_map/cond/branch_0_fun/rd,rqc->qdc/dot_general | solution.py:240
  681.1 9.4 %conditional.23 = (f32[4,3584,128]{1,2,0:T(8,128)}) conditional(s32[]{:T(128)} %convert_element_type.149, (bf16[512,4,128]{0,2,1:T(8,128)(2,1)S(1)}, bf16[512,3584]{1,0:T(8,128)(2,1)}, f32[4,3584,128]{1,2,0:T(8,128)}) %tuple.116, f32[4,3584,128]{1,2,0:T(8,128)} %get-tuple-element.323), branch_computations={%region_51.52_spmd, %region_52.53_spmd} | conditional | flops 1880883200 | bytes 18874376 | solution.py:236
  681.1 9.4 %bitcast_add_fusion.2 = f32[4,3584,128]{1,2,0:T(8,128)} fusion(f32[4,3584,128]{1,2,0:T(8,128)} %get-tuple-element.117, bf16[512,4,128]{0,2,1:T(8,128)(2,1)S(1)} %get-tuple-element.118, bf16[512,3584]{1,0:T(8,128)(2,1)} %get-tuple-element.119), kind=kOutput, calls=%fused_computation.6 | convolution fusion | flops 1880883200 | bytes 18874368 | tf_op jit(solution)/shard_map/cond/branch_0_fun/rd,rqc->qdc/dot_general | solution.py:240
  690.5 8.4 %copy.52 = f32[4,3584,128]{2,1,0:T(8,128)} copy(f32[4,3584,128]{1,2,0:T(8,128)} %get-tuple-element.324) | data formatting | bytes 14680064 | tf_op jit(solution)/shard_map/cond | solution.py:236
  (325 shorter events, 293.3 us)
Async XLA Ops:
  13.5 87.1 %all-to-all-start.1 = ((bf16[16,32,5120]{2,1,0:T(8,128)(2,1)}), bf16[16,32,5120]{2,1,0:T(8,128)(2,1)}, u32[]{:S(2)}, u32[]{:S(2)}) async-start(bf16[16,32,5120]{2,1,0:T(8,128)(2,1)} %stack.27), calls=%async_computation.1 | async-start | bytes 10485760 | tf_op jit(solution)/shard_map/all_to_all | solution.py:165
  21.6 492.4 %all-gather.5.cloned.1.call-start = ((), (), s32[]{:S(2)}) async-start(), calls=%async_computation.21 | async-start | bytes 4587520 | tf_op jit(solution)/shard_map/all_gather | solution.py:76
  103.6 103.9 %all-to-all-start.3 = ((bf16[16,32,5120]{2,1,0:T(8,128)(2,1)}), bf16[16,32,5120]{2,1,0:T(8,128)(2,1)}, u32[]{:S(2)}, u32[]{:S(2)}) async-start(bf16[16,32,5120]{2,1,0:T(8,128)(2,1)} %stack.30), calls=%async_computation.3 | async-start | bytes 10485760 | tf_op jit(solution)/shard_map/all_to_all | solution.py:165
  116.0 414.2 %all-gather.9.cloned.1.call-start = ((), (), s32[]{:S(2)}) async-start(), calls=%async_computation.23 | async-start | bytes 4587520 | tf_op jit(solution)/shard_map/all_gather | solution.py:76
  210.4 111.6 %all-to-all-start.5 = ((bf16[16,32,5120]{2,1,0:T(8,128)(2,1)}), bf16[16,32,5120]{2,1,0:T(8,128)(2,1)}, u32[]{:S(2)}, u32[]{:S(2)}) async-start(bf16[16,32,5120]{2,1,0:T(8,128)(2,1)} %stack.33), calls=%async_computation.5 | async-start | bytes 10485760 | tf_op jit(solution)/shard_map/all_to_all | solution.py:165
  220.5 321.0 %all-gather.7.cloned.1.call-start = ((), (), s32[]{:S(2)}) async-start(), calls=%async_computation.22 | async-start | bytes 4587520 | tf_op jit(solution)/shard_map/all_gather | solution.py:76
  325.0 135.9 %all-to-all-start.7 = ((bf16[16,32,5120]{2,1,0:T(8,128)(2,1)}), bf16[16,32,5120]{2,1,0:T(8,128)(2,1)}, u32[]{:S(2)}, u32[]{:S(2)}) async-start(bf16[16,32,5120]{2,1,0:T(8,128)(2,1)} %stack.36), calls=%async_computation.7 | async-start | bytes 10485760 | tf_op jit(solution)/shard_map/all_to_all | solution.py:165
  332.6 222.3 %all-gather.11.cloned.1.call-start = ((), (), s32[]{:S(2)}) async-start(), calls=%async_computation.24 | async-start | bytes 4587520 | tf_op jit(solution)/shard_map/all_gather | solution.py:76
  461.7 12.2 %all-to-all-start.4 = ((f32[16,1024,4]{1,2,0:T(4,128)}), f32[16,1024,4]{1,2,0:T(4,128)S(1)}, u32[]{:S(2)}, u32[]{:S(2)}) async-start(f32[16,1024,4]{1,2,0:T(4,128)} %broadcast_in_dim.27), calls=%async_computation.4 | async-start | bytes 524288 | tf_op jit(solution)/shard_map/all_to_all | solution.py:28
  474.7 12.8 %all-to-all-start.6 = ((f32[16,1024,4]{1,2,0:T(4,128)}), f32[16,1024,4]{1,2,0:T(4,128)}, u32[]{:S(2)}, u32[]{:S(2)}) async-start(f32[16,1024,4]{1,2,0:T(4,128)} %broadcast_in_dim.28), calls=%async_computation.6 | async-start | bytes 524288 | tf_op jit(solution)/shard_map/all_to_all | solution.py:28
  488.2 12.2 %all-to-all-start.8 = ((f32[16,1024,4]{1,2,0:T(4,128)}), f32[16,1024,4]{1,2,0:T(4,128)S(1)}, u32[]{:S(2)}, u32[]{:S(2)}) async-start(f32[16,1024,4]{1,2,0:T(4,128)} %broadcast_in_dim.29), calls=%async_computation.8 | async-start | bytes 524288 | tf_op jit(solution)/shard_map/all_to_all | solution.py:28
  501.1 12.0 %all-to-all-start.2 = ((f32[16,1024,4]{1,2,0:T(4,128)}), f32[16,1024,4]{1,2,0:T(4,128)S(1)}, u32[]{:S(2)}, u32[]{:S(2)}) async-start(f32[16,1024,4]{1,2,0:T(4,128)} %broadcast_in_dim.26), calls=%async_computation.2 | async-start | bytes 524288 | tf_op jit(solution)/shard_map/all_to_all | solution.py:28
  526.4 40.7 %all-to-all-start = ((f32[16,1536,4]{1,2,0:T(4,128)}), f32[16,1536,4]{1,2,0:T(4,128)S(1)}, u32[]{:S(2)}, u32[]{:S(2)}) async-start(f32[16,1536,4]{1,2,0:T(4,128)} %broadcast_in_dim.25), calls=%async_computation | async-start | bytes 786432 | tf_op jit(solution)/shard_map/all_to_all | solution.py:28
  568.7 18.7 %all-to-all-start.10 = ((f32[16,1536,4]{1,2,0:T(4,128)}), f32[16,1536,4]{1,2,0:T(4,128)}, u32[]{:S(2)}, u32[]{:S(2)}) async-start(f32[16,1536,4]{1,2,0:T(4,128)} %broadcast_in_dim.31), calls=%async_computation.10 | async-start | bytes 786432 | tf_op jit(solution)/shard_map/all_to_all | solution.py:28
  588.9 13.9 %all-to-all-start.11 = ((f32[16,1536,4]{1,2,0:T(4,128)}), f32[16,1536,4]{1,2,0:T(4,128)S(1)}, u32[]{:S(2)}, u32[]{:S(2)}) async-start(f32[16,1536,4]{1,2,0:T(4,128)} %broadcast_in_dim.32), calls=%async_computation.11 | async-start | bytes 786432 | tf_op jit(solution)/shard_map/all_to_all | solution.py:28
  604.4 12.9 %all-to-all-start.9 = ((f32[16,1536,4]{1,2,0:T(4,128)}), f32[16,1536,4]{1,2,0:T(4,128)S(1)}, u32[]{:S(2)}, u32[]{:S(2)}) async-start(f32[16,1536,4]{1,2,0:T(4,128)} %broadcast_in_dim.30), calls=%async_computation.9 | async-start | bytes 786432 | tf_op jit(solution)/shard_map/all_to_all | solution.py:28
  608.1 191.9 %reduce-scatter.2.cloned.1.call-start = ((), (), s32[]{:S(2)}) async-start(), calls=%async_computation.25 | async-start | bytes 8257536 | tf_op jit(solution)/shard_map/reduce_scatter | solution.py:247
  614.7 35.7 %collective-permute-start = (bf16[4,512,4,128]{1,3,2,0:T(8,128)(2,1)}, bf16[4,512,4,128]{1,3,2,0:T(8,128)(2,1)}, u32[]{:S(2)}, u32[]{:S(2)}) collective-permute-start(bf16[4,512,4,128]{1,3,2,0:T(8,128)(2,1)} %pad_maximum_fusion), channel_id=1, source_target_pairs={{0,64},{1,65},{2,66},{3,67},{4,68},{5,69},{6,70},{7,71},{8,72},{9,... | collective-permute-start | bytes 6291464 | tf_op jit(solution)/shard_map/ppermute | solution.py:83
  700.4 14.4 %all-to-all-start.14 = ((f32[16,1,128]{2,1,0:T(1,128)}), f32[16,1,128]{2,1,0:T(1,128)S(1)}, u32[]{:S(2)}, u32[]{:S(2)}) async-start(f32[16,1,128]{2,1,0:T(1,128)} %reshape.528), calls=%async_computation.15 | async-start | bytes 16384 | tf_op jit(solution)/shard_map/all_to_all | solution.py:69
  714.9 10.9 %all-to-all-start.16 = ((f32[16,1,128]{2,1,0:T(1,128)}), f32[16,1,128]{2,1,0:T(1,128)S(1)}, u32[]{:S(2)}, u32[]{:S(2)}) async-start(f32[16,1,128]{2,1,0:T(1,128)} %reshape.524), calls=%async_computation.17 | async-start | bytes 16384 | tf_op jit(solution)/shard_map/all_to_all | solution.py:69
  754.6 11.0 %all-to-all-start.19 = ((f32[16,1,128]{2,1,0:T(1,128)}), f32[16,1,128]{2,1,0:T(1,128)S(1)}, u32[]{:S(2)}, u32[]{:S(2)}) async-start(f32[16,1,128]{2,1,0:T(1,128)} %reshape.522), calls=%async_computation.20 | async-start | bytes 16384 | tf_op jit(solution)/shard_map/all_to_all | solution.py:69
  765.6 10.9 %all-to-all-start.17 = ((f32[16,1,128]{2,1,0:T(1,128)}), f32[16,1,128]{2,1,0:T(1,128)S(1)}, u32[]{:S(2)}, u32[]{:S(2)}) async-start(f32[16,1,128]{2,1,0:T(1,128)} %reshape.526), calls=%async_computation.18 | async-start | bytes 16384 | tf_op jit(solution)/shard_map/all_to_all | solution.py:69
  776.5 11.0 %all-to-all-start.15 = ((f32[16,1,128]{2,1,0:T(1,128)}), f32[16,1,128]{2,1,0:T(1,128)S(1)}, u32[]{:S(2)}, u32[]{:S(2)}) async-start(f32[16,1,128]{2,1,0:T(1,128)} %reshape.530), calls=%async_computation.16 | async-start | bytes 16384 | tf_op jit(solution)/shard_map/all_to_all | solution.py:69
  787.5 10.9 %all-to-all-start.13 = ((f32[16,1,128]{2,1,0:T(1,128)}), f32[16,1,128]{2,1,0:T(1,128)S(1)}, u32[]{:S(2)}, u32[]{:S(2)}) async-start(f32[16,1,128]{2,1,0:T(1,128)} %reshape.534), calls=%async_computation.14 | async-start | bytes 16384 | tf_op jit(solution)/shard_map/all_to_all | solution.py:69
  (38 other events, 672.2 us)
Sparse Core Ops, SparseCore 0:
  89.5 112.7 all-gather.4
  204.0 100.5 all-gather.8
  306.2 77.0 all-gather.6
  384.9 67.3 all-gather.10
  699.1 46.4 reduce-scatter.1
